TPU v7x, 256 devices: a whole 4x4x8 slice. The times are simulated.
256 devices in a mesh: depth: 4 (over x), row: 16 (over z, y_hi), col: 4 (over y_lo, core).
Axes of the slice: x: 4, y: 4 (y_hi: 2, y_lo: 2; y = y_hi * 2 + y_lo), z: 8, core: 2. Of those that a mesh axis runs over, the one named last changes fastest.
Arguments:
- tokens: bfloat16 [768, 8192], P(('depth', 'row')), may hold values from -6 to 6
- out_grad: bfloat16 [768, 8192], P(('depth', 'row')), may hold values from -0.59765625 to 0.59765625
- gate_weight: bfloat16 [8192, 16384], P('depth', ('row', 'col')), may hold values from -0.0625 to 0.0625
- up_weight: bfloat16 [8192, 16384], P('depth', ('row', 'col')), may hold values from -0.0625 to 0.0625
- down_weight: bfloat16 [16384, 8192], P(('row', 'col'), 'depth'), may hold values from -0.046875 to 0.046875
Outputs:
- input_grad: bfloat16 [768, 8192], P(('depth', 'row', 'col'))
- gate_grad: bfloat16 [8192, 16384], P('depth', ('row', 'col'))
- up_grad: bfloat16 [8192, 16384], P('depth', ('row', 'col'))
- down_grad: bfloat16 [16384, 8192], P(('row', 'col'), 'depth')
All inputs are finite; a program needn't handle non-finite values.
Results may differ from a plain program's by a relative error of at most 0.024.
Values may be sent and summed in bfloat16 or wider, within the bound.
No kernel may reach another device: no remote copies, remote signals or barrier semaphores. Data moves between devices by JAX's collectives and lax.ppermute only.
A program may use at most 128 MiB of HBM per device.

v0:
```python
import jax
import jax.numpy as jnp
from jax import lax
from jax.sharding import PartitionSpec as P


def contract_rows(left, right):
    return lax.dot_general(
        left, right, (((0,), (0,)), ((), ())), preferred_element_type=jnp.float32
    )


def contract_cols(left, right):
    return lax.dot_general(
        left, right, (((1,), (1,)), ((), ())), preferred_element_type=jnp.float32
    )


def swiglu_terms(gate, up, hidden_grad):
    sig = jax.nn.sigmoid(gate)
    act = gate * sig
    hidden = (act * up).astype(jnp.bfloat16)
    gate_term = (hidden_grad * up * sig * (1.0 + gate * (1.0 - sig))).astype(jnp.bfloat16)
    up_term = (hidden_grad * act).astype(jnp.bfloat16)
    return (hidden, gate_term, up_term)


def block_work(tok_part, grad_part, gate_full, up_full, down_full):
    gate = jnp.dot(tok_part, gate_full, preferred_element_type=jnp.float32)
    up = jnp.dot(tok_part, up_full, preferred_element_type=jnp.float32)
    hidden_grad = contract_cols(grad_part, down_full)
    hidden, gate_term, up_term = swiglu_terms(gate, up, hidden_grad)
    partial_in = contract_cols(gate_term, gate_full) + contract_cols(up_term, up_full)
    return (hidden, gate_term, up_term, partial_in)


def on_device(tokens, out_grad, gate_weight, up_weight, down_weight):
    gate_full, up_full, down_full = (
        lax.all_gather(gate_weight, "depth", axis=0, tiled=True),
        lax.all_gather(up_weight, "depth", axis=0, tiled=True),
        lax.all_gather(down_weight, "depth", axis=1, tiled=True),
    )
    all_tok, all_grad = (
        lax.all_gather(tokens, "row", axis=0, tiled=True),
        lax.all_gather(out_grad, "row", axis=0, tiled=True),
    )
    hidden, gate_term, up_term, partial_in = block_work(
        all_tok, all_grad, gate_full, up_full, down_full
    )
    input_grad = lax.psum_scatter(
        partial_in, ("row", "col"), scatter_dimension=0, tiled=True
    ).astype(jnp.bfloat16)
    gate_grad, up_grad, down_grad = (
        lax.psum_scatter(
            contract_rows(all_tok, gate_term).astype(jnp.bfloat16),
            "depth",
            scatter_dimension=0,
            tiled=True,
        ).astype(jnp.float32),
        lax.psum_scatter(
            contract_rows(all_tok, up_term).astype(jnp.bfloat16),
            "depth",
            scatter_dimension=0,
            tiled=True,
        ).astype(jnp.float32),
        lax.psum_scatter(
            contract_rows(hidden, all_grad).astype(jnp.bfloat16),
            "depth",
            scatter_dimension=1,
            tiled=True,
        ).astype(jnp.float32),
    )
    return (
        input_grad,
        gate_grad.astype(jnp.bfloat16),
        up_grad.astype(jnp.bfloat16),
        down_grad.astype(jnp.bfloat16),
    )


def solution(mesh):
    return jax.shard_map(
        on_device,
        mesh=mesh,
        in_specs=(
            P(("depth", "row"), None),
            P(("depth", "row"), None),
            P("depth", ("row", "col")),
            P("depth", ("row", "col")),
            P(("row", "col"), "depth"),
        ),
        out_specs=(
            P(("depth", "row", "col"), None),
            P("depth", ("row", "col")),
            P("depth", ("row", "col")),
            P(("row", "col"), "depth"),
        ),
        check_vma=False,
    )
```

profile of v0, /device:TPU:2, one launch (start us, length us, event | category | flops | bytes accessed | tf_op | source)
XLA Modules:
  0.0 703.7 jit_solution(15544658315042769333)
XLA Ops:
  7.2 0.7 all-gather.16.cloned.1.call-update
  7.9 0.7 all-gather.14.cloned.1.call-update
  8.7 0.7 all-gather.10.cloned.1.call-update
  10.6 103.0 %all-gather.16.cloned.1.call-done = bf16[16,12,8192]{2,1,0:T(8,128)(2,1)} async-done(((bf16[1,12,8192]{2,1,0:T(8,128)(2,1)}), bf16[16,12,8192]{2,1,0:T(8,128)(2,1)}) %all-gather.16.cloned.1.call-update) | async-done | bytes 3145744 | tf_op jit(solution)/shard_map/all_gather | solution.py:44
  113.6 3.2 reshape.11
  116.9 95.9 %all-gather.14.cloned.1.call-done = bf16[16,12,8192]{2,1,0:T(8,128)(2,1)} async-done(((bf16[1,12,8192]{2,1,0:T(8,128)(2,1)}), bf16[16,12,8192]{2,1,0:T(8,128)(2,1)}) %all-gather.14.cloned.1.call-update) | async-done | bytes 3145744 | tf_op jit(solution)/shard_map/all_gather | solution.py:45
  212.7 4.7 reshape.9
  217.4 43.8 %all-gather.10.cloned.1.call-done = bf16[8192,256]{1,0:T(8,128)(2,1)} async-done(((bf16[2048,256]{1,0:T(8,128)(2,1)}), bf16[8192,256]{1,0:T(8,128)(2,1)}) %all-gather.10.cloned.1.call-update) | async-done | bytes 4194320 | tf_op jit(solution)/shard_map/all_gather | solution.py:40
  261.3 3.2 fusion.5
  264.4 49.7 %all-gather.12.cloned.1.call-done = bf16[8192,256]{1,0:T(8,128)(2,1)} async-done(((bf16[2048,256]{1,0:T(8,128)(2,1)}), bf16[8192,256]{1,0:T(8,128)(2,1)}) %all-gather.12.cloned.1.call-update) | async-done | bytes 4194320 | tf_op jit(solution)/shard_map/all_gather | solution.py:39
  314.1 3.2 fusion.6
  317.3 49.7 %all-gather.8.cloned.1.call-done = bf16[256,8192]{1,0:T(8,128)(2,1)} async-done(((bf16[256,2048]{1,0:T(8,128)(2,1)}), bf16[256,8192]{1,0:T(8,128)(2,1)}) %all-gather.8.cloned.1.call-update) | async-done | bytes 4194320 | tf_op jit(solution)/shard_map/all_gather | solution.py:41
  367.0 5.3 multiply_convert_fusion.1
  372.3 0.6 copy-done.3
  373.0 3.2 fusion.1
  376.2 4.2 fusion
  380.5 1.8 copy-done.1
  382.3 3.3 convolution_convert_fusion
  386.8 4.4 fusion.7
  391.2 4.2 convolution_add_fusion
  395.4 296.2 %all-reduce.2 = bf16[192,8192]{1,0:T(8,128)(2,1)S(1)} all-reduce(f32[192,8192]{1,0:T(8,128)} %convolution_add_fusion), channel_id=2, replica_groups=mesh['depth'=4,'row'=16,'col'=4] {'row','col'}, use_global_device_ids=true, to_apply=%region_0.0.clone | all-reduce | flops 1572864 | bytes 9437184
  691.6 0.7 dynamic-slice_convert_fusion
  692.3 2.3 copy.14
  694.6 2.3 copy.13
  (27 shorter events, 2.0 us)
Async XLA Ops:
  7.2 106.4 %all-gather.16.cloned.1.call-start = ((), (), s32[]{:S(2)}) async-start(), calls=%async_computation.10 | async-start | bytes 4456448 | tf_op jit(solution)/shard_map/all_gather | solution.py:44
  7.9 204.8 %all-gather.14.cloned.1.call-start = ((), (), s32[]{:S(2)}) async-start(), calls=%async_computation.9 | async-start | bytes 4456448 | tf_op jit(solution)/shard_map/all_gather | solution.py:45
  8.6 252.6 %all-gather.10.cloned.1.call-start = ((), (), s32[]{:S(2)}) async-start(), calls=%async_computation.4 | async-start | bytes 5242880 | tf_op jit(solution)/shard_map/all_gather | solution.py:40
  9.4 304.7 %all-gather.12.cloned.1.call-start = ((), (), s32[]{:S(2)}) async-start(), calls=%async_computation.5 | async-start | bytes 5242880 | tf_op jit(solution)/shard_map/all_gather | solution.py:39
  10.0 357.0 %all-gather.8.cloned.1.call-start = ((), (), s32[]{:S(2)}) async-start(), calls=%async_computation.3 | async-start | bytes 5242880 | tf_op jit(solution)/shard_map/all_gather | solution.py:41
  10.5 681.7 %reduce-scatter.6.cloned.1.call-start = ((), (), s32[]{:S(2)}) async-start(), calls=%async_computation.7 | async-start | bytes 5242880 | tf_op jit(solution)/shard_map/reduce_scatter | solution.py:60
  372.3 0.6 copy-start.3
  376.2 318.4 %reduce-scatter.4.cloned.1.call-start = ((), (), s32[]{:S(2)}) async-start(), calls=%async_computation.6 | async-start | bytes 5242880 | tf_op jit(solution)/shard_map/reduce_scatter | solution.py:54
  380.4 1.9 copy-start.1
  380.4 5.1 copy-start.5
  380.4 316.4 %reduce-scatter.8.cloned.1.call-start = ((), (), s32[]{:S(2)}) async-start(), calls=%async_computation.8 | async-start | bytes 5242880 | tf_op jit(solution)/shard_map/reduce_scatter | solution.py:66
  385.5 1.3 copy-start.2
  386.8 4.4 copy-start
  386.8 4.4 copy-start.4
Sparse Core Ops, SparseCore 0:
  10.6 102.9 all-gather.15
  116.2 96.5 all-gather.13
  214.6 46.6 all-gather.9
  262.9 51.1 all-gather.11
  315.8 51.1 all-gather.7
  376.3 49.0 reduce-scatter.5
  428.2 49.0 reduce-scatter.3
  480.4 49.0 reduce-scatter.7
where the time goes:
time: 704 us
  waiting for transfers between devices  345 us (49%)
  blocking collectives  296 us (42%)
  matrix products  30.8 us (4%)
  local copies, waits for them, and re-layouts  16.2 us (2%)
  between operations  14.9 us (2%)
    unnamed x1, blocking collectives  296 us
    all_gather x1, waiting for transfers between devices, on_device(): lax.all_gather(tokens, 'row', axis=0, tiled=True)  103 us
    all_gather x1, waiting for transfers between devices, on_device(): lax.all_gather(out_grad, 'row', axis=0, tiled=True)  95.9 us
    all_gather x1, waiting for transfers between devices, on_device(): lax.all_gather(gate_weight, 'depth', axis=0, tiled=True)  49.7 us
    all_gather x1, waiting for transfers between devices, on_device(): lax.all_gather(down_weight, 'depth', axis=1, tiled=True)  49.7 us
    all_gather x1, waiting for transfers between devices, on_device(): lax.all_gather(up_weight, 'depth', axis=0, tiled=True)  43.8 us
    unnamed x17, local copies, waits for them, and re-layouts  15.5 us
  transfers between devices with their start and end apart: 8, of which 5 were waited for; matrix products, arithmetic and copies ran while one was open for 5% of the time, Pallas kernels for 0%

commit v1 on v0

--- a/solution.py
+++ b/solution.py
@@ -2,6 +2,13 @@
 import jax.numpy as jnp
 from jax import lax
 from jax.sharding import PartitionSpec as P
+
+
+def all_by_exchange(x, axis, d):
+    size = lax.axis_size(axis)
+    tiles = jnp.stack([x for _ in range(size)])
+    tiles = lax.all_to_all(tiles, axis, split_axis=0, concat_axis=0)
+    return jnp.concatenate(tiles, axis=d)
 
 
 def contract_rows(left, right):
@@ -36,7 +43,7 @@
 
 def on_device(tokens, out_grad, gate_weight, up_weight, down_weight):
     gate_full, up_full, down_full = (
-        lax.all_gather(gate_weight, "depth", axis=0, tiled=True),
+        all_by_exchange(gate_weight, "depth", 0),
         lax.all_gather(up_weight, "depth", axis=0, tiled=True),
         lax.all_gather(down_weight, "depth", axis=1, tiled=True),
     )

time: 704 us -> 651 us (0.925)
  waiting for transfers between devices: 345 us -> 282 us
    all_gather x1 -> x0, waiting for transfers between devices: 49.7 us -> none  [on_device(): lax.all_gather(gate_weight, 'depth', axis=0, tiled=True)]
    all_gather x1, waiting for transfers between devices: 103 us -> 93.1 us  [on_device(): lax.all_gather(tokens, 'row', axis=0, tiled=True)]
    all_to_all x0 -> x1, starting transfers between devices: none -> 7.07 us  [all_by_exchange(): tiles = lax.all_to_all(tiles, axis, split_axis=0, concat_axis=0)]
  transfers between devices with their start and end apart: 8 -> 8, of which waited for: 5 -> 4; matrix products, arithmetic and copies ran while one was open for 5% -> 6% of each run, Pallas kernels for 0% -> 0%
where the time goes in v1:
time: 651 us
  blocking collectives  296 us (45%)
  waiting for transfers between devices  282 us (43%)
  matrix products  30.8 us (5%)
  local copies, waits for them, and re-layouts  19.7 us (3%)
  between operations  14.9 us (2%)
  starting transfers between devices  7.31 us (1%)
    unnamed x1, blocking collectives  296 us
    all_gather x1, waiting for transfers between devices, on_device(): lax.all_gather(out_grad, 'row', axis=0, tiled=True)  95.9 us
    all_gather x1, waiting for transfers between devices, on_device(): lax.all_gather(tokens, 'row', axis=0, tiled=True)  93.1 us
    all_gather x1, waiting for transfers between devices, on_device(): lax.all_gather(down_weight, 'depth', axis=1, tiled=True)  49.7 us
    all_gather x1, waiting for transfers between devices, on_device(): lax.all_gather(up_weight, 'depth', axis=0, tiled=True)  40.6 us
    unnamed x17, local copies, waits for them, and re-layouts  15.5 us
    dot_general x3, matrix products, contract_cols(): lax.dot_general(left, right, (((1,), (1,)), ((), ())), preferred_element_...  13.8 us
  transfers between devices with their start and end apart: 8, of which 4 were waited for; matrix products, arithmetic and copies ran while one was open for 6% of the time, Pallas kernels for 0%

profile of v1, /device:TPU:2, one launch (start us, length us, event | category | flops | bytes accessed | tf_op | source)
XLA Modules:
  0.0 650.8 jit_solution(3058405788610709587)
XLA Ops:
  7.2 0.7 all-gather.13.cloned.1.call-update
  7.9 0.7 all-gather.11.cloned.1.call-update
  8.7 0.7 all-gather.9.cloned.1.call-update
  10.0 3.5 stack.2
  13.4 7.1 %all-to-all-start = ((bf16[4,2048,256]{2,1,0:T(8,128)(2,1)}), bf16[4,2048,256]{2,1,0:T(8,128)(2,1)}, u32[]{:S(2)}, u32[]{:S(2)}) async-start(bf16[4,2048,256]{2,1,0:T(8,128)(2,1)} %stack.2), calls=%async_computation | async-start | bytes 8388608 | tf_op jit(solution)/shard_map/all_to_all | solution.py:10
  20.5 93.1 %all-gather.13.cloned.1.call-done = bf16[16,12,8192]{2,1,0:T(8,128)(2,1)} async-done(((bf16[1,12,8192]{2,1,0:T(8,128)(2,1)}), bf16[16,12,8192]{2,1,0:T(8,128)(2,1)}) %all-gather.13.cloned.1.call-update) | async-done | bytes 3145744 | tf_op jit(solution)/shard_map/all_gather | solution.py:51
  113.6 3.2 reshape.17
  116.9 95.9 %all-gather.11.cloned.1.call-done = bf16[16,12,8192]{2,1,0:T(8,128)(2,1)} async-done(((bf16[1,12,8192]{2,1,0:T(8,128)(2,1)}), bf16[16,12,8192]{2,1,0:T(8,128)(2,1)}) %all-gather.11.cloned.1.call-update) | async-done | bytes 3145744 | tf_op jit(solution)/shard_map/all_gather | solution.py:52
  212.7 4.7 reshape.15
  217.4 3.2 fusion.6
  220.6 40.6 %all-gather.9.cloned.1.call-done = bf16[8192,256]{1,0:T(8,128)(2,1)} async-done(((bf16[2048,256]{1,0:T(8,128)(2,1)}), bf16[8192,256]{1,0:T(8,128)(2,1)}) %all-gather.9.cloned.1.call-update) | async-done | bytes 4194320 | tf_op jit(solution)/shard_map/all_gather | solution.py:47
  261.3 3.2 fusion.5
  264.4 49.7 %all-gather.7.cloned.1.call-done = bf16[256,8192]{1,0:T(8,128)(2,1)} async-done(((bf16[256,2048]{1,0:T(8,128)(2,1)}), bf16[256,8192]{1,0:T(8,128)(2,1)}) %all-gather.7.cloned.1.call-update) | async-done | bytes 4194320 | tf_op jit(solution)/shard_map/all_gather | solution.py:48
  314.1 5.3 multiply_convert_fusion.1
  320.1 3.2 fusion
  323.4 4.1 fusion.1
  327.6 1.8 copy-done.1
  329.4 3.3 convolution_convert_fusion
  334.0 4.3 fusion.7
  338.3 4.2 convolution_add_fusion
  342.5 296.2 %all-reduce.2 = bf16[192,8192]{1,0:T(8,128)(2,1)S(1)} all-reduce(f32[192,8192]{1,0:T(8,128)} %convolution_add_fusion), channel_id=2, replica_groups=mesh['depth'=4,'row'=16,'col'=4] {'row','col'}, use_global_device_ids=true, to_apply=%region_0.0.clone | all-reduce | flops 1572864 | bytes 9437184
  638.7 0.7 dynamic-slice_convert_fusion
  639.4 2.3 copy.13
  641.7 2.3 copy.14
  (27 shorter events, 2.1 us)
Async XLA Ops:
  7.2 106.4 %all-gather.13.cloned.1.call-start = ((), (), s32[]{:S(2)}) async-start(), calls=%async_computation.10 | async-start | bytes 4456448 | tf_op jit(solution)/shard_map/all_gather | solution.py:51
  7.9 204.8 %all-gather.11.cloned.1.call-start = ((), (), s32[]{:S(2)}) async-start(), calls=%async_computation.9 | async-start | bytes 4456448 | tf_op jit(solution)/shard_map/all_gather | solution.py:52
  8.6 252.6 %all-gather.9.cloned.1.call-start = ((), (), s32[]{:S(2)}) async-start(), calls=%async_computation.5 | async-start | bytes 5242880 | tf_op jit(solution)/shard_map/all_gather | solution.py:47
  9.4 304.7 %all-gather.7.cloned.1.call-start = ((), (), s32[]{:S(2)}) async-start(), calls=%async_computation.4 | async-start | bytes 5242880 | tf_op jit(solution)/shard_map/all_gather | solution.py:48
  13.4 204.0 %all-to-all-start = ((bf16[4,2048,256]{2,1,0:T(8,128)(2,1)}), bf16[4,2048,256]{2,1,0:T(8,128)(2,1)}, u32[]{:S(2)}, u32[]{:S(2)}) async-start(bf16[4,2048,256]{2,1,0:T(8,128)(2,1)} %stack.2), calls=%async_computation | async-start | bytes 8388608 | tf_op jit(solution)/shard_map/all_to_all | solution.py:10
  20.5 618.9 %reduce-scatter.4.cloned.1.call-start = ((), (), s32[]{:S(2)}) async-start(), calls=%async_computation.6 | async-start | bytes 5242880 | tf_op jit(solution)/shard_map/reduce_scatter | solution.py:61
  319.5 0.6 copy-start.2
  323.4 318.3 %reduce-scatter.6.cloned.1.call-start = ((), (), s32[]{:S(2)}) async-start(), calls=%async_computation.7 | async-start | bytes 5242880 | tf_op jit(solution)/shard_map/reduce_scatter | solution.py:67
  327.5 1.9 copy-start.1
  327.5 5.2 copy-start.5
  327.5 316.4 %reduce-scatter.8.cloned.1.call-start = ((), (), s32[]{:S(2)}) async-start(), calls=%async_computation.8 | async-start | bytes 5242880 | tf_op jit(solution)/shard_map/reduce_scatter | solution.py:73
  332.7 1.3 copy-start.3
  333.9 4.3 copy-start
  334.0 4.3 copy-start.4
Sparse Core Ops, SparseCore 0:
  10.6 102.9 all-gather.12
  116.2 96.5 all-gather.10
  214.6 46.6 all-gather.8
  262.9 51.1 all-gather.6
  323.5 49.0 reduce-scatter.3
  375.2 49.0 reduce-scatter.5
  427.4 49.0 reduce-scatter.7
